TPU v7x, 512 devices: a whole 4x8x8 slice. The times are simulated.
512 devices in a mesh: row: 16 (over y, z_lo), col: 32 (over z_hi, x, core).
Axes of the slice: x: 4, y: 8, z: 8 (z_hi: 4, z_lo: 2; z = z_hi * 2 + z_lo), core: 2. Of those that a mesh axis runs over, the one named last changes fastest.
Arguments:
- tiles: bfloat16 [16, 32, 32, 256, 256], P('row', 'col'), may hold values from -6 to 6
- tile_ids: int32 [16, 32, 2, 32], P('row', 'col'), may hold values from 0 to 7, as said below
- tile_count: int32 [16, 32], P('row', 'col'), may hold values from 8 to 32
- query_degree: int32 [32768], P('row'), may hold values from 1 to 32
- product_degree: int32 [65536], P('col'), may hold values from 1 to 32
- panel: float32 [64, 65536], P(None, ('col', 'row')), may hold values from -6 to 6
Outputs:
- basis: float32 [64, 65536], P(None, ('col', 'row'))
Inputs may be any that keep to these rules, and one draw needn't show every extreme that they name: `tile_ids`: on each device the 32 (tile row, tile column) pairs are distinct; tile row is below 8 and tile column below 8.
All inputs are finite; a program needn't handle non-finite values.
Results may differ from a plain program's by a relative error of at most 0.0042.
Values may be sent and summed in bfloat16 or wider, within the bound.
A program may use at most 64 MiB of HBM per device.

v0:
```python
import math
import jax
import jax.numpy as jnp
from jax import lax
from jax.sharding import PartitionSpec as P

ITERS = 2
HIGH = lax.Precision.HIGHEST


def orthonormal(lifted, gram):
    lower = jnp.linalg.cholesky(gram)
    return lax.linalg.triangular_solve(lower, lifted, left_side=True, lower=True)


def shards(tiles, tile_ids, tile_count, query_degree, product_degree, panel):
    tile_set = tiles[0, 0]
    slot_ids = tile_ids[0, 0]
    live_count = tile_count[0, 0]
    slots = tile_set.shape[0]
    side = tile_set.shape[1]
    width = panel.shape[0]
    query_tiles = query_degree.shape[0] // side
    product_tiles = product_degree.shape[0] // side
    live_slot = (jnp.arange(slots, dtype=jnp.int32) < live_count).astype(jnp.float32)
    row_hot = (slot_ids[0][:, None] == jnp.arange(query_tiles, dtype=jnp.int32)[None, :]).astype(
        jnp.float32
    ) * live_slot[:, None]
    col_hot = (slot_ids[1][:, None] == jnp.arange(product_tiles, dtype=jnp.int32)[None, :]).astype(
        jnp.float32
    ) * live_slot[:, None]
    qscale = 1.0 / jnp.sqrt(query_degree.astype(jnp.float32))
    pscale = 1.0 / jnp.sqrt(product_degree.astype(jnp.float32))
    row_at = lax.axis_index("row")
    col_at = lax.axis_index("col")
    share = panel.shape[1]
    my_pscale = lax.dynamic_slice_in_dim(pscale, row_at * share, share)
    root_count = math.sqrt(product_degree.shape[0] * lax.axis_size("col"))
    current = panel
    for iteration in range(ITERS):
        scaled = (current * my_pscale[None, :]).astype(jnp.bfloat16)
        scaled_block = lax.all_gather(scaled, "row", axis=1, tiled=True)
        picked = jnp.take(scaled_block.reshape(width, product_tiles, side), slot_ids[1], axis=1)
        products = jnp.einsum("rkj,kij->kri", picked, tile_set, preferred_element_type=jnp.float32)
        partial_sum = jnp.einsum("kq,kri->rqi", row_hot, products, precision=HIGH).reshape(
            width, query_tiles * side
        )
        query_share = lax.psum_scatter(partial_sum, "col", scatter_dimension=1, tiled=True)
        columns = query_share.shape[1]
        my_qscale = lax.dynamic_slice_in_dim(qscale, col_at * columns, columns)
        rounded = (query_share * my_qscale[None, :]).astype(jnp.bfloat16)
        query_block = lax.all_gather(rounded, "col", axis=1, tiled=True)
        backward_picked = jnp.take(
            query_block.reshape(width, query_tiles, side), slot_ids[0], axis=1
        )
        backward_products = jnp.einsum(
            "rki,kij->krj", backward_picked, tile_set, preferred_element_type=jnp.float32
        )
        lifted = (
            lax.psum_scatter(
                jnp.einsum("kp,krj->rpj", col_hot, backward_products, precision=HIGH).reshape(
                    width, product_tiles * side
                ),
                "row",
                scatter_dimension=1,
                tiled=True,
            )
            * my_pscale[None, :]
        )
        gram = lax.psum(jnp.einsum("ri,si->rs", lifted, lifted, precision=HIGH), ("row", "col"))
        current = orthonormal(lifted, gram)
    return current * root_count


def solution(mesh):
    in_specs = (
        P("row", "col", None, None, None),
        P("row", "col", None, None),
        P("row", "col"),
        P("row"),
        P("col"),
        P(None, ("col", "row")),
    )
    out_specs = P(None, ("col", "row"))
    return jax.shard_map(shards, mesh=mesh, in_specs=in_specs, out_specs=out_specs, check_vma=False)
```

profile of v0, /device:TPU:24, one launch (start us, length us, event | category | flops | bytes accessed | tf_op | source)
XLA Modules:
  0.0 757.7 jit_solution(1532699937566994767)
XLA Ops:
  6.5 0.8 slice_bitcast_fusion.1
  7.3 0.8 compare_and_fusion
  8.7 0.8 fusion.78
  9.5 0.8 multiply_convert_fusion.2
  10.3 32.3 %all_gather.12 = bf16[64,2048]{1,0:T(8,128)(2,1)S(1)} all-gather(bf16[64,128]{1,0:T(8,128)(2,1)S(1)} %multiply_convert_fusion.2), channel_id=1, replica_groups=mesh['row'=16,'col'=32] {'row'}, dimensions={1}, use_global_device_ids=true | all-gather | bytes 278528 | tf_op jit(solution)/shard_map/all_gather | solution.py:42
  42.6 0.6 gather_fusion
  43.2 3.6 fusion.6
  46.8 2.4 fusion.16
  49.1 1.4 copy.55
  50.6 0.8 fusion.77
  51.3 101.7 %reduce-scatter.13.cloned.1.call-done = f32[64,64]{1,0:T(8,128)} async-done(((f32[2048,64]{1,0:T(8,128)}), f32[64,64]{1,0:T(8,128)}) %reduce-scatter.13.cloned.1.call-update) | async-done | bytes 16400
  153.1 0.8 copy.52
  153.9 0.1 copy.31
  154.0 43.8 %all_gather.13 = bf16[64,2048]{0,1:T(8,128)(2,1)S(1)} all-gather(bf16[64,64]{0,1:T(8,128)(2,1)S(1)} %copy.31), channel_id=1, replica_groups=mesh['row'=16,'col'=32] {'col'}, dimensions={1}, use_global_device_ids=true | all-gather | bytes 270336 | tf_op jit(solution)/shard_map/all_gather | solution.py:52
  197.8 0.2 copy.33
  198.0 0.6 gather_fusion.1
  198.6 3.1 fusion.4
  201.7 2.4 fusion.12
  204.1 1.0 copy.59
  205.1 67.3 %reduce-scatter.9.cloned.1.call-done = f32[64,128]{1,0:T(8,128)} async-done(((f32[64,2048]{1,0:T(8,128)}), f32[64,128]{1,0:T(8,128)}) %reduce-scatter.9.cloned.1.call-update) | async-done | bytes 32784 | tf_op jit(solution)/shard_map/reduce_scatter | solution.py:60
  272.4 1.0 fusion.51
  273.4 98.9 %psum.14 = f32[64,64]{0,1:T(8,128)S(1)} all-reduce(f32[64,64]{0,1:T(8,128)S(1)} %fusion.51), channel_id=1, replica_groups=mesh['row'=16,'col'=32] {'row','col'}, use_global_device_ids=true, to_apply=%region_2.4 | all-reduce | flops 4096 | bytes 32768 | tf_op jit(solution)/shard_map/psum | solution.py:70
  372.5 5.8 cholesky.44
  378.3 0.6 compare_reduce_fusion.1
  379.0 0.7 fusion.39
  379.6 4.9 custom-call.6
  384.5 1.0 fusion.22
  385.6 29.2 %all_gather.14 = bf16[64,2048]{1,0:T(8,128)(2,1)S(1)} all-gather(bf16[64,128]{1,0:T(8,128)(2,1)S(1)} %fusion.22), channel_id=1, replica_groups=mesh['row'=16,'col'=32] {'row'}, dimensions={1}, use_global_device_ids=true | all-gather | bytes 278528 | tf_op jit(solution)/shard_map/all_gather | solution.py:42
  414.8 0.6 gather_fusion.2
  415.4 3.6 fusion.2
  419.0 2.4 fusion.19
  421.4 1.4 copy.56
  422.8 95.3 %reduce-scatter.15.cloned.1.call-done = f32[64,64]{1,0:T(8,128)} async-done(((f32[2048,64]{1,0:T(8,128)}), f32[64,64]{1,0:T(8,128)}) %reduce-scatter.15.cloned.1.call-update) | async-done | bytes 16400
  518.1 0.8 copy.54
  519.0 43.8 %all_gather.15 = bf16[64,2048]{0,1:T(8,128)(2,1)S(1)} all-gather(bf16[64,64]{0,1:T(8,128)(2,1)S(1)} %copy.39), channel_id=1, replica_groups=mesh['row'=16,'col'=32] {'col'}, dimensions={1}, use_global_device_ids=true | all-gather | bytes 270336 | tf_op jit(solution)/shard_map/all_gather | solution.py:52
  562.8 0.2 copy.41
  563.0 0.6 gather_fusion.3
  563.6 3.1 fusion
  566.7 2.4 fusion.8
  569.1 1.0 copy.60
  570.1 67.3 %reduce-scatter.11.cloned.1.call-done = f32[64,128]{1,0:T(8,128)} async-done(((f32[64,2048]{1,0:T(8,128)}), f32[64,128]{1,0:T(8,128)}) %reduce-scatter.11.cloned.1.call-update) | async-done | bytes 32784 | tf_op jit(solution)/shard_map/reduce_scatter | solution.py:60
  637.4 1.0 fusion.48
  638.4 99.0 %psum.15 = f32[64,64]{0,1:T(8,128)S(1)} all-reduce(f32[64,64]{0,1:T(8,128)S(1)} %fusion.48), channel_id=1, replica_groups=mesh['row'=16,'col'=32] {'row','col'}, use_global_device_ids=true, to_apply=%region_7.11 | all-reduce | flops 4096 | bytes 32768 | tf_op jit(solution)/shard_map/psum | solution.py:70
  737.5 5.8 cholesky.55
  743.4 0.6 compare_reduce_fusion
  744.0 0.7 fusion.40
  744.7 4.9 custom-call.7
  749.6 1.6 convolution_multiply_fusion
  (22 shorter events, 0.6 us)
Async XLA Ops:
  6.5 146.5 %reduce-scatter.13.cloned.1.call-start = ((), (), s32[]{:S(2)}) async-start(), calls=%async_computation.6 | async-start | bytes 1081344
  50.5 221.9 %reduce-scatter.9.cloned.1.call-start = ((), (), s32[]{:S(2)}) async-start(), calls=%async_computation.4 | async-start | bytes 557056 | tf_op jit(solution)/shard_map/reduce_scatter | solution.py:60
  205.0 313.1 %reduce-scatter.15.cloned.1.call-start = ((), (), s32[]{:S(2)}) async-start(), calls=%async_computation.7 | async-start | bytes 1081344
  422.8 214.6 %reduce-scatter.11.cloned.1.call-start = ((), (), s32[]{:S(2)}) async-start(), calls=%async_computation.5 | async-start | bytes 557056 | tf_op jit(solution)/shard_map/reduce_scatter | solution.py:60
Sparse Core Ops, SparseCore 0:
  50.6 102.3 reduce-scatter.12
  205.2 67.2 reduce-scatter.8
  422.9 95.1 reduce-scatter.14
  570.2 67.1 reduce-scatter.10
where the time goes:
time: 759 us; the launch traced here: 758 us
  blocking collectives  347 us (46%)
  waiting for transfers between devices  332 us (44%)
  matrix products  27.4 us (4%)
  other arithmetic  27.3 us (4%)
  between operations  14 us (2%)
  local copies, waits for them, and re-layouts  10.3 us (1%)
    psum x2, blocking collectives, shards(): lax.psum(jnp.einsum('ri,si->rs', lifted, lifted, precision=HIGH), ('row',...  198 us
    unnamed x6, waiting for transfers between devices  197 us
    reduce_scatter x2, waiting for transfers between devices, shards(): lax.psum_scatter(jnp.einsum('kp,krj->rpj', col_hot, backward_products, pr...  135 us
    all_gather x2, blocking collectives, shards(): query_block = lax.all_gather(rounded, 'col', axis=1, tiled=True)  87.6 us
    all_gather x2, blocking collectives, shards(): scaled_block = lax.all_gather(scaled, 'row', axis=1, tiled=True)  61.5 us
  transfers between devices with their start and end apart: 4, of which 4 were waited for; matrix products, arithmetic and copies ran while one was open for 0% of the time, Pallas kernels for 0%

commit v1 on v0

--- a/solution.py
+++ b/solution.py
@@ -67,7 +67,9 @@
             )
             * my_pscale[None, :]
         )
-        gram = lax.psum(jnp.einsum("ri,si->rs", lifted, lifted, precision=HIGH), ("row", "col"))
+        gram = jnp.einsum("ri,si->rs", lifted, lifted, precision=HIGH)
+        for mesh_axis in ("row", "col"):
+            gram = lax.psum(gram, mesh_axis)
         current = orthonormal(lifted, gram)
     return current * root_count
 

time: 759 us -> 966 us (1.27)
  the two profiles are of different devices: /device:TPU:24 before, /device:TPU:32 now
where the time goes in v1:
time: 966 us; the launch traced here: 965 us
  blocking collectives  555 us (57%)
  waiting for transfers between devices  332 us (34%)
  matrix products  27.4 us (3%)
  other arithmetic  27.2 us (3%)
  between operations  14 us (1%)
  local copies, waits for them, and re-layouts  10.3 us (1%)
    psum x4, blocking collectives, shards(): gram = lax.psum(gram, mesh_axis)  402 us
    unnamed x6, waiting for transfers between devices  197 us
    reduce_scatter x2, waiting for transfers between devices, shards(): lax.psum_scatter(jnp.einsum('kp,krj->rpj', col_hot, backward_products, pr...  135 us
    all_gather x2, blocking collectives, shards(): query_block = lax.all_gather(rounded, 'col', axis=1, tiled=True)  87.6 us
    all_gather x2, blocking collectives, shards(): scaled_block = lax.all_gather(scaled, 'row', axis=1, tiled=True)  64.6 us
  transfers between devices with their start and end apart: 4, of which 4 were waited for; matrix products, arithmetic and copies ran while one was open for 0% of the time, Pallas kernels for 0%

profile of v1, /device:TPU:32, one launch (start us, length us, event | category | flops | bytes accessed | tf_op | source)
XLA Modules:
  0.0 965.4 jit_solution(9216616157615196403)
XLA Ops:
  6.5 0.8 slice_bitcast_fusion.1
  7.3 0.8 compare_and_fusion
  8.7 0.8 fusion.78
  9.5 0.8 multiply_convert_fusion.2
  10.3 33.4 %all_gather.12 = bf16[64,2048]{1,0:T(8,128)(2,1)S(1)} all-gather(bf16[64,128]{1,0:T(8,128)(2,1)S(1)} %multiply_convert_fusion.2), channel_id=1, replica_groups=mesh['row'=16,'col'=32] {'row'}, dimensions={1}, use_global_device_ids=true | all-gather | bytes 278528 | tf_op jit(solution)/shard_map/all_gather | solution.py:42
  43.7 0.6 gather_fusion
  44.3 3.6 fusion.6
  47.9 2.4 fusion.16
  50.2 1.4 copy.55
  51.7 0.8 fusion.77
  52.4 100.5 %reduce-scatter.13.cloned.1.call-done = f32[64,64]{1,0:T(8,128)} async-done(((f32[2048,64]{1,0:T(8,128)}), f32[64,64]{1,0:T(8,128)}) %reduce-scatter.13.cloned.1.call-update) | async-done | bytes 16400
  153.0 0.8 copy.52
  153.9 43.8 %all_gather.13 = bf16[64,2048]{0,1:T(8,128)(2,1)S(1)} all-gather(bf16[64,64]{0,1:T(8,128)(2,1)S(1)} %copy.31), channel_id=1, replica_groups=mesh['row'=16,'col'=32] {'col'}, dimensions={1}, use_global_device_ids=true | all-gather | bytes 270336 | tf_op jit(solution)/shard_map/all_gather | solution.py:52
  197.7 0.2 copy.33
  197.9 0.6 gather_fusion.1
  198.5 3.1 fusion.4
  201.6 2.4 fusion.12
  203.9 1.0 copy.59
  205.0 67.3 %reduce-scatter.9.cloned.1.call-done = f32[64,128]{1,0:T(8,128)} async-done(((f32[64,2048]{1,0:T(8,128)}), f32[64,128]{1,0:T(8,128)}) %reduce-scatter.9.cloned.1.call-update) | async-done | bytes 32784 | tf_op jit(solution)/shard_map/reduce_scatter | solution.py:60
  272.3 1.0 fusion.51
  273.3 62.2 %psum.28 = f32[64,64]{0,1:T(8,128)S(1)} all-reduce(f32[64,64]{0,1:T(8,128)S(1)} %fusion.51), channel_id=1, replica_groups=mesh['row'=16,'col'=32] {'row'}, use_global_device_ids=true, to_apply=%region_2.4 | all-reduce | flops 4096 | bytes 32768 | tf_op jit(solution)/shard_map/psum | solution.py:72
  335.5 139.0 %psum.29 = f32[64,64]{0,1:T(8,128)S(1)} all-reduce(f32[64,64]{0,1:T(8,128)S(1)} %psum.28), channel_id=1, replica_groups=mesh['row'=16,'col'=32] {'col'}, use_global_device_ids=true, to_apply=%region_3.5 | all-reduce | flops 4096 | bytes 32768 | tf_op jit(solution)/shard_map/psum | solution.py:72
  474.6 5.8 cholesky.44
  480.5 0.6 compare_reduce_fusion.1
  481.1 0.7 fusion.39
  481.8 4.9 custom-call.6
  486.7 1.0 fusion.22
  487.7 31.2 %all_gather.14 = bf16[64,2048]{1,0:T(8,128)(2,1)S(1)} all-gather(bf16[64,128]{1,0:T(8,128)(2,1)S(1)} %fusion.22), channel_id=1, replica_groups=mesh['row'=16,'col'=32] {'row'}, dimensions={1}, use_global_device_ids=true | all-gather | bytes 278528 | tf_op jit(solution)/shard_map/all_gather | solution.py:42
  518.9 0.6 gather_fusion.2
  519.5 3.6 fusion.2
  523.1 2.4 fusion.19
  525.5 1.4 copy.56
  526.9 96.6 %reduce-scatter.15.cloned.1.call-done = f32[64,64]{1,0:T(8,128)} async-done(((f32[2048,64]{1,0:T(8,128)}), f32[64,64]{1,0:T(8,128)}) %reduce-scatter.15.cloned.1.call-update) | async-done | bytes 16400
  623.5 0.8 copy.54
  624.4 43.8 %all_gather.15 = bf16[64,2048]{0,1:T(8,128)(2,1)S(1)} all-gather(bf16[64,64]{0,1:T(8,128)(2,1)S(1)} %copy.39), channel_id=1, replica_groups=mesh['row'=16,'col'=32] {'col'}, dimensions={1}, use_global_device_ids=true | all-gather | bytes 270336 | tf_op jit(solution)/shard_map/all_gather | solution.py:52
  668.5 0.6 gather_fusion.3
  669.1 3.1 fusion
  672.2 2.4 fusion.8
  674.5 1.0 copy.60
  675.5 67.4 %reduce-scatter.11.cloned.1.call-done = f32[64,128]{1,0:T(8,128)} async-done(((f32[64,2048]{1,0:T(8,128)}), f32[64,128]{1,0:T(8,128)}) %reduce-scatter.11.cloned.1.call-update) | async-done | bytes 32784 | tf_op jit(solution)/shard_map/reduce_scatter | solution.py:60
  742.9 1.0 fusion.48
  743.9 62.1 %psum.30 = f32[64,64]{0,1:T(8,128)S(1)} all-reduce(f32[64,64]{0,1:T(8,128)S(1)} %fusion.48), channel_id=1, replica_groups=mesh['row'=16,'col'=32] {'row'}, use_global_device_ids=true, to_apply=%region_8.0 | all-reduce | flops 4096 | bytes 32768 | tf_op jit(solution)/shard_map/psum | solution.py:72
  806.0 139.0 %psum.31 = f32[64,64]{0,1:T(8,128)S(1)} all-reduce(f32[64,64]{0,1:T(8,128)S(1)} %psum.30), channel_id=1, replica_groups=mesh['row'=16,'col'=32] {'col'}, use_global_device_ids=true, to_apply=%region_9.13 | all-reduce | flops 4096 | bytes 32768 | tf_op jit(solution)/shard_map/psum | solution.py:72
  945.2 5.8 cholesky.55
  951.0 0.6 compare_reduce_fusion
  951.7 0.7 fusion.40
  952.3 4.9 custom-call.7
  957.2 1.6 convolution_multiply_fusion
  (24 shorter events, 0.9 us)
Async XLA Ops:
  6.5 146.4 %reduce-scatter.13.cloned.1.call-start = ((), (), s32[]{:S(2)}) async-start(), calls=%async_computation.6 | async-start | bytes 1081344
  51.6 220.7 %reduce-scatter.9.cloned.1.call-start = ((), (), s32[]{:S(2)}) async-start(), calls=%async_computation.4 | async-start | bytes 557056 | tf_op jit(solution)/shard_map/reduce_scatter | solution.py:60
  204.9 418.6 %reduce-scatter.15.cloned.1.call-start = ((), (), s32[]{:S(2)}) async-start(), calls=%async_computation.7 | async-start | bytes 1081344
  526.8 216.0 %reduce-scatter.11.cloned.1.call-start = ((), (), s32[]{:S(2)}) async-start(), calls=%async_computation.5 | async-start | bytes 557056 | tf_op jit(solution)/shard_map/reduce_scatter | solution.py:60
Sparse Core Ops, SparseCore 0:
  51.7 101.1 reduce-scatter.12
  205.0 67.1 reduce-scatter.8
  527.0 96.4 reduce-scatter.14
  675.6 67.2 reduce-scatter.10
